TPU v7x, 32 devices: a whole 2x2x4 slice. The times are simulated.
32 devices in a mesh: rows: 8 (over y, x, core), cols: 4 (over z).
Axes of the slice: x: 2, y: 2, z: 4, core: 2. Of those that a mesh axis runs over, the one named last changes fastest.
Arguments:
- grads: bfloat16 [9216, 8192], P(('rows', 'cols')), may hold values from -6 to 6
- tests: float32 [64, 8192], P(None, 'cols'), may hold values from -6 to 6
Outputs:
- solution: float32 [64, 8192], P(None, 'cols')
- scores: float32 [64, 9216], P(None, ('rows', 'cols'))
All inputs are finite; a program needn't handle non-finite values.
Results may differ from a plain program's by a relative error of at most 0.0041.
Values may be sent and summed in bfloat16 or wider, within the bound.
A program may use at most 64 MiB of HBM per device.

v0:
```python
import jax
import jax.numpy as jnp
from jax import lax
from jax.sharding import PartitionSpec as P

damping = 0.5


def per_device(grads, tests):
    n_total = grads.shape[0] * lax.axis_size("rows") * lax.axis_size("cols")
    width = grads.shape[1]
    own = tests.shape[1]
    direction = lax.all_gather(tests, "cols", axis=1, tiled=True)
    norm_now = jnp.sum(direction * direction, axis=1)

    def project(d):
        return lax.dot_general(
            grads,
            d.astype(jnp.bfloat16),
            (((1,), (1,)), ((), ())),
            preferred_element_type=jnp.float32,
        )

    partial_value = lax.dot_general(
        project(direction).astype(jnp.bfloat16),
        grads,
        (((0,), (0,)), ((), ())),
        preferred_element_type=jnp.float32,
    )
    image = lax.psum(partial_value, ("rows", "cols")) / n_total + damping * direction
    alpha = norm_now / jnp.sum(direction * image, axis=1)
    solution = alpha[:, None] * direction
    residual = direction - alpha[:, None] * image
    norm_next = jnp.sum(residual * residual, axis=1)
    direction = residual + (norm_next / norm_now)[:, None] * direction
    proj = project(direction)
    curv = lax.psum(
        jnp.sum(proj * proj.astype(jnp.bfloat16).astype(jnp.float32), axis=0), ("rows", "cols")
    )
    curv = curv / n_total + damping * jnp.sum(direction * direction, axis=1)
    solution = solution + (norm_next / curv)[:, None] * direction
    scores = lax.dot_general(
        solution.astype(jnp.bfloat16),
        grads,
        (((1,), (1,)), ((), ())),
        preferred_element_type=jnp.float32,
    )
    mine = lax.dynamic_slice_in_dim(solution, lax.axis_index("cols") * own, own, axis=1)
    return (mine, scores * width ** (-0.5))


def solution(mesh):
    placed = (P(("rows", "cols"), None), P(None, "cols"))
    return jax.shard_map(
        per_device,
        mesh=mesh,
        in_specs=placed,
        out_specs=(P(None, "cols"), P(None, ("rows", "cols"))),
        check_vma=False,
    )
```

profile of v0, /device:TPU:0, one launch (start us, length us, event | category | flops | bytes accessed | tf_op | source)
XLA Modules:
  0.0 261.7 jit_solution(16199284651384448593)
XLA Ops:
  7.2 0.0 all-gather.2.cloned.1.call-start
  7.2 0.7 all-gather.2.cloned.1.call-update
  7.9 0.0 all-reduce.2.cloned.1.call-start
  7.9 50.0 %all-gather.2.cloned.1.call-done = f32[64,8192]{1,0:T(8,128)} async-done(((f32[64,2048]{1,0:T(8,128)}), f32[64,8192]{1,0:T(8,128)}) %all-gather.2.cloned.1.call-update) | async-done | bytes 2097168 | tf_op jit(solution)/shard_map/all_gather | solution.py:13
  58.0 9.7 %fusion = f32[64,8192]{1,0:T(8,128)} fusion(bf16[288,8192]{1,0:T(8,128)(2,1)} %param.2, f32[64,8192]{1,0:T(8,128)} %all-gather.2.cloned.1.call-done), kind=kOutput, calls=%fused_computation.11 | convolution fusion | flops 604522496 | bytes 8912896 | tf_op jit(solution)/shard_map/dot_general | solution.py:24
  67.6 0.0 copy-start
  67.6 0.0 all-reduce.2.cloned.1.call-update
  67.7 133.7 %all-reduce.2.cloned.1.call-done = f32[64,8192]{1,0:T(8,128)} async-done(((f32[64,8192]{1,0:T(8,128)}), f32[64,8192]{1,0:T(8,128)}) %all-reduce.2.cloned.1.call-update) | async-done | bytes 2097168 | tf_op jit(solution)/shard_map/psum | solution.py:30
  201.4 0.0 copy-done
  201.4 0.0 copy-start.1
  201.4 2.3 multiply_reduce_fusion.2
  203.7 0.0 copy-start.2
  203.7 2.3 multiply_reduce_fusion.1
  206.1 0.0 copy-done.1
  206.1 0.0 copy-done.2
  206.1 0.0 slice-start
  206.1 1.8 multiply_reduce_fusion.4
  207.9 38.9 %psum.15 = f32[64]{0:T(128)S(1)} all-reduce(f32[64]{0:T(128)S(1)} %multiply_reduce_fusion.4), channel_id=1, replica_groups=mesh['rows'=8,'cols'=4] {'rows','cols'}, use_global_device_ids=true, to_apply=%region_5.0 | all-reduce | flops 64 | bytes 512 | tf_op jit(solution)/shard_map/psum | solution.py:37
  246.9 2.5 multiply_reduce_fusion
  249.4 2.3 multiply_add_fusion
  251.7 0.0 slice-done
  251.7 0.0 slice-done.1
  251.7 2.3 convolution_multiply_fusion
  254.0 0.8 constant_dynamic-slice_fusion
  (5 shorter events, 0.0 us)
Async XLA Ops:
  7.2 50.8 %all-gather.2.cloned.1.call-start = ((), (), s32[]{:S(2)}) async-start(), calls=%async_computation | async-start | bytes 2621440 | tf_op jit(solution)/shard_map/all_gather | solution.py:13
  7.9 193.5 %all-reduce.2.cloned.1.call-start = ((), (), s32[]{:S(2)}) async-start(), calls=%async_computation.1 | async-start | bytes 4194304 | tf_op jit(solution)/shard_map/psum | solution.py:30
  67.6 133.7 %copy-start = (f32[64,8192]{1,0:T(8,128)S(1)}, f32[64,8192]{1,0:T(8,128)}, u32[]{:S(2)}) copy-start(f32[64,8192]{1,0:T(8,128)} %all-gather.2.cloned.1.call-done) | copy-start | bytes 6291460
  201.4 4.7 %copy-start.1 = (bf16[288,8192]{1,0:T(8,128)(2,1)S(1)}, bf16[288,8192]{1,0:T(8,128)(2,1)}, u32[]{:S(2)}) copy-start(bf16[288,8192]{1,0:T(8,128)(2,1)} %param.2) | copy-start | bytes 14155780
  203.7 2.4 copy-start.2
  206.1 45.6 %slice-start = ((s8[4718592]{0:T(1024)(128)(4,1)}), s8[524288]{0:T(1024)(128)(4,1)S(1)}, s32[]{:S(2)}) async-start(s8[4718592]{0:T(1024)(128)(4,1)} %bitcast.8), calls=%async_computation.2 | async-start | bytes 1048576
  246.9 4.8 %slice-start.1 = ((s8[4718592]{0:T(1024)(128)(4,1)}), s8[4194304]{0:T(1024)(128)(4,1)S(1)}, s32[]{:S(2)}) async-start(s8[4718592]{0:T(1024)(128)(4,1)} %bitcast.8), calls=%async_computation.3 | async-start | bytes 8388608
Sparse Core Ops, SparseCore 0:
  9.5 48.3 all-gather.1
  67.8 133.5 all-reduce.1
where the time goes:
time: 262 us
  waiting for transfers between devices  184 us (70%)
  blocking collectives  38.9 us (15%)
  between operations  14.1 us (5%)
  matrix products  13.8 us (5%)
  other arithmetic  9.47 us (4%)
    psum x1, waiting for transfers between devices, per_device(): lax.psum(partial_value, ('rows', 'cols')) / n_total + damping * direction  134 us
    all_gather x1, waiting for transfers between devices, per_device(): direction = lax.all_gather(tests, 'cols', axis=1, tiled=True)  50 us
    psum x1, blocking collectives, per_device(): lax.psum(jnp.sum(proj * proj.astype(jnp.bfloat16).astype(jnp.float32), ax...  38.9 us
    dot_general x1, matrix products, per_device(): lax.dot_general(project(direction).astype(jnp.bfloat16), grads, (((0,), (...  9.67 us
  transfers between devices with their start and end apart: 2, of which 2 were waited for; matrix products, arithmetic and copies ran while one was open for 0% of the time, Pallas kernels for 0%

commit v1 on v0

--- a/solution.py
+++ b/solution.py
@@ -6,11 +6,29 @@
 damping = 0.5
 
 
+def in_order(parts, dim):
+    shape = list(parts.shape[1:])
+    shape[dim] *= parts.shape[0]
+    return jnp.moveaxis(parts, 0, dim).reshape(shape)
+
+
+def doubled(x, axis):
+    size = lax.axis_size(axis)
+    blocks = x[None]
+    for level in range(size.bit_length() - 1):
+        apart = 1 << level
+        theirs = lax.ppermute(blocks, axis, [(i, i ^ apart) for i in range(size)])
+        both = jnp.stack([blocks, theirs])
+        upper = lax.axis_index(axis) >> level & 1
+        blocks = jnp.where(upper == 0, both, both[::-1]).reshape(-1, *x.shape)
+    return blocks
+
+
 def per_device(grads, tests):
     n_total = grads.shape[0] * lax.axis_size("rows") * lax.axis_size("cols")
     width = grads.shape[1]
     own = tests.shape[1]
-    direction = lax.all_gather(tests, "cols", axis=1, tiled=True)
+    direction = in_order(doubled(tests, "cols"), 1)
     norm_now = jnp.sum(direction * direction, axis=1)
 
     def project(d):

time: 262 us -> 282 us (1.076)
  waiting for transfers between devices: 184 us -> 190 us
  starting transfers between devices: 0.08 us -> 5.97 us
  matrix products: 13.8 us -> 18 us
    ppermute x0 -> x2, waiting for transfers between devices: none -> 57.1 us  [doubled(): theirs = lax.ppermute(blocks, axis, [(i, i ^ apart) for i in range(size)])]
    all_gather x1 -> x0, waiting for transfers between devices: 50 us -> none  [per_device(): direction = lax.all_gather(tests, 'cols', axis=1, tiled=True)]
    ppermute x0 -> x2, starting transfers between devices: none -> 5.94 us  [doubled(): theirs = lax.ppermute(blocks, axis, [(i, i ^ apart) for i in range(size)])]
    reduce_sum x0 -> x1, other arithmetic: none -> 3.15 us  [per_device(): norm_now = jnp.sum(direction * direction, axis=1)]
  transfers between devices with their start and end apart: 2 -> 3, of which waited for: 2 -> 3; matrix products, arithmetic and copies ran while one was open for 0% -> 1% of each run, Pallas kernels for 0% -> 0%
where the time goes in v1:
time: 282 us; the launch traced here: 281 us
  waiting for transfers between devices  190 us (67%)
  blocking collectives  39.1 us (14%)
  matrix products  18 us (6%)
  between operations  14.1 us (5%)
  other arithmetic  11 us (4%)
  starting transfers between devices  5.97 us (2%)
  local copies, waits for them, and re-layouts  3.41 us (1%)
    psum x1, waiting for transfers between devices, per_device(): lax.psum(partial_value, ('rows', 'cols')) / n_total + damping * direction  133 us
    ppermute x2, waiting for transfers between devices, doubled(): theirs = lax.ppermute(blocks, axis, [(i, i ^ apart) for i in range(size)])  57.1 us
    psum x1, blocking collectives, per_device(): lax.psum(jnp.sum(proj * proj.astype(jnp.bfloat16).astype(jnp.float32), ax...  39.1 us
    dot_general x1, matrix products, per_device(): lax.dot_general(project(direction).astype(jnp.bfloat16), grads, (((0,), (...  9.23 us
    ppermute x2, starting transfers between devices, doubled(): theirs = lax.ppermute(blocks, axis, [(i, i ^ apart) for i in range(size)])  5.94 us
  transfers between devices with their start and end apart: 3, of which 3 were waited for; matrix products, arithmetic and copies ran while one was open for 1% of the time, Pallas kernels for 0%

profile of v1, /device:TPU:0, one launch (start us, length us, event | category | flops | bytes accessed | tf_op | source)
XLA Modules:
  0.0 281.4 jit_solution(2368959386913164923)
XLA Ops:
  7.2 0.0 all-reduce.2.cloned.1.call-start
  7.2 3.1 %collective-permute-start = (f32[1,64,2048]{2,1,0:T(8,128)}, f32[1,64,2048]{2,1,0:T(8,128)S(1)}, u32[]{:S(2)}, u32[]{:S(2)}) collective-permute-start(f32[1,64,2048]{2,1,0:T(8,128)} %bitcast.33), channel_id=1, source_target_pairs={{0,1},{1,0},{2,3},{3,2},{4,5},{5,4},{6,7},{7,6},{8,9},{9,8},{10,11... | collective-permute-start | bytes 1572872 | tf_op jit(solution)/shard_map/ppermute | solution.py:20
  10.3 12.1 %collective-permute-done = f32[1,64,2048]{2,1,0:T(8,128)S(1)} collective-permute-done((f32[1,64,2048]{2,1,0:T(8,128)}, f32[1,64,2048]{2,1,0:T(8,128)S(1)}, u32[]{:S(2)}, u32[]{:S(2)}) %collective-permute-start) | collective-permute-done | bytes 524320 | tf_op jit(solution)/shard_map/ppermute | solution.py:20
  22.5 1.1 pad_maximum_fusion.1
  23.6 0.2 fusion.7
  23.8 2.8 %collective-permute-start.1 = (f32[2,64,2048]{2,1,0:T(8,128)S(1)}, f32[2,64,2048]{2,1,0:T(8,128)S(1)}, u32[]{:S(2)}, u32[]{:S(2)}) collective-permute-start(f32[2,64,2048]{2,1,0:T(8,128)S(1)} %get-tuple-element.3), channel_id=1, source_target_pairs={{0,2},{1,3},{2,0},{3,1},{4,6},{5,7},{6,4},{7,5},{8,10},{9,11},{10,... | collective-permute-start | bytes 3145736 | tf_op jit(solution)/shard_map/ppermute | solution.py:20
  26.6 44.9 %collective-permute-done.1 = f32[2,64,2048]{2,1,0:T(8,128)S(1)} collective-permute-done((f32[2,64,2048]{2,1,0:T(8,128)S(1)}, f32[2,64,2048]{2,1,0:T(8,128)S(1)}, u32[]{:S(2)}, u32[]{:S(2)}) %collective-permute-start.1) | collective-permute-done | bytes 1048608 | tf_op jit(solution)/shard_map/ppermute | solution.py:20
  71.6 0.2 pad_maximum_fusion
  71.8 0.2 reverse_select_fusion
  72.0 1.4 copy.4
  73.4 1.2 copy.5
  74.6 9.2 %fusion.1 = f32[64,8192]{1,0:T(8,128)} fusion(bf16[288,8192]{1,0:T(8,128)(2,1)} %param.2, f32[64,8192]{1,0:T(8,128)S(1)} %bitcast.23), kind=kOutput, calls=%fused_computation.15 | convolution fusion | flops 604522496 | bytes 8912896 | tf_op jit(solution)/shard_map/dot_general | solution.py:42
  83.8 0.0 all-reduce.2.cloned.1.call-update
  83.8 3.2 %fusion = f32[64]{0:T(128)S(1)} fusion(f32[4,64,2048]{2,1,0:T(8,128)} %bitcast.30), kind=kLoop, calls=%fused_computation.3 | loop fusion | flops 1048512 | bytes 2097408 | tf_op jit(solution)/shard_map/reduce_sum | solution.py:32
  87.0 132.6 %all-reduce.2.cloned.1.call-done = f32[64,8192]{1,0:T(8,128)} async-done(((f32[64,8192]{1,0:T(8,128)}), f32[64,8192]{1,0:T(8,128)}) %all-reduce.2.cloned.1.call-update) | async-done | bytes 2097168 | tf_op jit(solution)/shard_map/psum | solution.py:48
  219.6 2.2 multiply_reduce_fusion.2
  221.8 0.0 copy-done
  221.8 0.7 multiply_reduce_fusion.1
  222.5 4.2 %multiply_reduce_fusion.3 = f32[64]{0:T(128)S(1)} fusion(bf16[288,8192]{1,0:T(8,128)(2,1)} %param.2, f32[64,8192]{1,0:T(8,128)S(1)} %bitcast.26, f32[64,8192]{1,0:T(8,128)S(1)} %copy-done, f32[64]{0:T(128)S(1)} %div.32, f32[64]{0:T(128)S(1)} %div.31), kind=kOutput, calls=%fused_computation.22 | convolution fusion | flops 306257856 | bytes 8913664 | tf_op jit(solution)/shard_map/dot_general | solution.py:35
  226.7 39.1 %psum.15 = f32[64]{0:T(128)S(1)} all-reduce(f32[64]{0:T(128)S(1)} %multiply_reduce_fusion.3), channel_id=1, replica_groups=mesh['rows'=8,'cols'=4] {'rows','cols'}, use_global_device_ids=true, to_apply=%region_5.6 | all-reduce | flops 64 | bytes 512 | tf_op jit(solution)/shard_map/psum | solution.py:55
  265.8 2.5 multiply_reduce_fusion
  268.3 0.7 multiply_add_fusion
  269.1 4.6 %convolution_multiply_fusion = f32[64,288]{1,0:T(8,128)} fusion(bf16[288,8192]{1,0:T(8,128)(2,1)} %param.2, f32[64,8192]{1,0:T(8,128)S(1)} %multiply_add_fusion), kind=kOutput, calls=%fused_computation.12 | convolution fusion | flops 302532608 | bytes 6889472 | tf_op jit(solution)/shard_map/dot_general | solution.py:60
  273.7 0.8 constant_dynamic-slice_fusion
  (8 shorter events, 0.0 us)
Async XLA Ops:
  7.2 212.4 %all-reduce.2.cloned.1.call-start = ((), (), s32[]{:S(2)}) async-start(), calls=%async_computation | async-start | bytes 4194304 | tf_op jit(solution)/shard_map/psum | solution.py:48
  7.2 15.3 %collective-permute-start = (f32[1,64,2048]{2,1,0:T(8,128)}, f32[1,64,2048]{2,1,0:T(8,128)S(1)}, u32[]{:S(2)}, u32[]{:S(2)}) collective-permute-start(f32[1,64,2048]{2,1,0:T(8,128)} %bitcast.33), channel_id=1, source_target_pairs={{0,1},{1,0},{2,3},{3,2},{4,5},{5,4},{6,7},{7,6},{8,9},{9,8},{10,11... | collective-permute-start | bytes 1572872 | tf_op jit(solution)/shard_map/ppermute | solution.py:20
  23.8 47.8 %collective-permute-start.1 = (f32[2,64,2048]{2,1,0:T(8,128)S(1)}, f32[2,64,2048]{2,1,0:T(8,128)S(1)}, u32[]{:S(2)}, u32[]{:S(2)}) collective-permute-start(f32[2,64,2048]{2,1,0:T(8,128)S(1)} %get-tuple-element.3), channel_id=1, source_target_pairs={{0,2},{1,3},{2,0},{3,1},{4,6},{5,7},{6,4},{7,5},{8,10},{9,11},{10,... | collective-permute-start | bytes 3145736 | tf_op jit(solution)/shard_map/ppermute | solution.py:20
  72.0 1.4 copy-start.2
  219.6 2.2 copy-start
  265.8 2.5 copy-start.1
Sparse Core Ops, SparseCore 0:
  84.0 135.6 all-reduce.1
